TPU v7x, 32 devices: a whole 2x2x4 slice. The times are simulated.
32 devices in a mesh: ctx: 4 (over z), head: 8 (over y, x, core).
Axes of the slice: x: 2, y: 2, z: 4, core: 2. Of those that a mesh axis runs over, the one named last changes fastest.
Arguments:
- layer_input: bfloat16 [1024, 4096], P(('ctx', 'head')), may hold values from -6 to 6
- w_query: bfloat16 [4096, 4096], P('ctx', 'head'), may hold values from -0.09375 to 0.09375
- w_key: bfloat16 [4096, 4096], P('ctx', 'head'), may hold values from -0.09375 to 0.09375
- w_value: bfloat16 [4096, 4096], P('ctx', 'head'), may hold values from -0.09375 to 0.09375
- w_out: bfloat16 [4096, 4096], P('head'), may hold values from -0.09375 to 0.09375
- log_decay: float32 [32, 1024], P('head', 'ctx'), may hold values from -2 to 0
- level_gain: float32 [32, 10], P('head'), may hold values from 0.5 to 2
- level_mask: int32 [8, 10], P('ctx'), may hold values 0 or 1
Outputs:
- layer_out: bfloat16 [1024, 4096], P(('ctx', 'head'))
All inputs are finite; a program needn't handle non-finite values. No bound on the sum of `level_mask` on one device may be relied on, other than what follows from the above.
Results may differ from a plain program's by a relative error of at most 0.023.
Values may be sent and summed in bfloat16 or wider, within the bound.
A program may use at most 64 MiB of HBM per device.

v0:
```python
import jax
import jax.numpy as jnp
from jax import lax
from jax.sharding import PartitionSpec as P

HEAD_DIM = 128
BLOCK = 128


def swapped(value, axis, stride):
    mask = 2**stride
    pairs = [(source, source ^ mask) for source in range(lax.axis_size(axis))]
    return lax.ppermute(value, axis, pairs)


def levels_of(first, second, count):
    mixed = jnp.bitwise_xor(first, second)
    result = jnp.zeros(mixed.shape, jnp.int32)
    for level_bit in range(count):
        result = result + (mixed >= 2**level_bit).astype(jnp.int32)
    return result


def unit_rows(block):
    floated = block.astype(jnp.float32)
    return (floated / jnp.sqrt(jnp.sum(floated * floated, axis=-1, keepdims=True) + 1e-06)).astype(
        jnp.bfloat16
    )


def on_device(layer_input, w_query, w_key, w_value, w_out, log_decay, level_gain, level_mask):
    full_query, full_key, full_value = (
        lax.all_gather(w_query, "ctx", axis=0, tiled=True),
        lax.all_gather(w_key, "ctx", axis=0, tiled=True),
        lax.all_gather(w_value, "ctx", axis=0, tiled=True),
    )
    piece = lax.all_gather(layer_input, "head", axis=0, tiled=True)
    outputs = [
        jnp.dot(piece, weight, preferred_element_type=jnp.float32).astype(jnp.bfloat16)
        for weight in (full_query, full_key, full_value)
    ]
    joined = jnp.concatenate(outputs, axis=1)
    width = full_query.shape[1]
    local_heads = width // HEAD_DIM
    span = joined.shape[0]
    query_unit = unit_rows(joined[:, :width].reshape(span, local_heads, HEAD_DIM))
    key_unit = unit_rows(joined[:, width : 2 * width].reshape(span, local_heads, HEAD_DIM))
    values = joined[:, 2 * width :].reshape(span, local_heads, HEAD_DIM)
    cum = jnp.cumsum(log_decay, axis=1)
    span_total = cum[:, -1]
    level_count = level_gain.shape[1]
    per_span = span // BLOCK
    ctx_index = lax.axis_index("ctx")
    blocks = ctx_index * per_span + jnp.arange(per_span, dtype=jnp.int32)
    level_range = jnp.arange(level_count, dtype=jnp.int32)
    near_levels = levels_of(blocks[:, None], blocks[None, :], level_count)
    near_onehot = (near_levels[..., None] == level_range).astype(jnp.float32)
    block_weight = level_mask.astype(jnp.float32)[:, None, :] * level_gain[None, :, :]
    near_block = jnp.einsum("bhl,bel->hbe", block_weight, near_onehot)
    scores = jnp.einsum("thd,shd->hts", query_unit, key_unit, preferred_element_type=jnp.float32)
    position = jnp.arange(span, dtype=jnp.int32)
    causal = position[:, None] >= position[None, :]
    spread = cum[:, :, None] - cum[:, None, :]
    decay_factor = jnp.where(causal, jnp.exp(jnp.where(causal, spread, 0.0)), 0.0)
    shaped = (scores * decay_factor).reshape(local_heads, per_span, BLOCK, per_span, BLOCK)
    near_weight = (
        (shaped * near_block[:, :, None, :, None])
        .reshape(local_heads, span, span)
        .astype(jnp.bfloat16)
    )
    near_out = jnp.einsum("hts,shd->thd", near_weight, values, preferred_element_type=jnp.float32)
    decayed_key = (
        key_unit.astype(jnp.float32) * jnp.exp(span_total[None, :] - cum.T)[:, :, None]
    ).astype(jnp.bfloat16)
    span_state = jnp.einsum("thd,the->hde", decayed_key, values, preferred_element_type=jnp.float32)
    bit_count = lax.axis_size("ctx").bit_length() - 1
    bit_range = jnp.arange(bit_count, dtype=jnp.int32)
    powers = jnp.left_shift(jnp.ones_like(bit_range), bit_range)
    group_total, group_state = (span_total, span_state)
    before = jnp.zeros_like(span_total)
    collected = []
    for bit_index in range(bit_count):
        other_total, other_state = (
            swapped(group_total.astype(jnp.bfloat16), "ctx", bit_index).astype(group_total.dtype),
            swapped(group_state.astype(jnp.bfloat16), "ctx", bit_index).astype(group_state.dtype),
        )
        upper = jnp.bitwise_and(jnp.right_shift(ctx_index, bit_index), 1) == 1
        collected.append(jnp.where(upper, jnp.exp(before)[:, None, None] * other_state, 0.0))
        lower_total = jnp.where(upper, other_total, group_total)
        higher_total = jnp.where(upper, group_total, other_total)
        lower_state = jnp.where(upper, other_state, group_state)
        higher_state = jnp.where(upper, group_state, other_state)
        group_state = jnp.exp(higher_total)[:, None, None] * lower_state + higher_state
        group_total = lower_total + higher_total
        before = before + jnp.where(upper, other_total, 0.0)
    carried = jnp.stack(collected, axis=0)
    partner = jnp.bitwise_xor(ctx_index, powers)
    far_levels = levels_of(blocks[:, None], (partner * per_span)[None, :], level_count)
    far_onehot = (far_levels[..., None] == level_range).astype(jnp.float32)
    far_block = jnp.einsum("bhl,bml->bhm", block_weight, far_onehot)
    far_tokens = jnp.repeat(far_block, BLOCK, axis=0)
    scaled = query_unit.astype(jnp.float32) * jnp.exp(cum.T)[:, :, None]
    reached = jnp.einsum("thd,mhde->thme", scaled, carried, precision=lax.Precision.HIGHEST)
    far_out = jnp.einsum("thme,thm->the", reached, far_tokens, precision=lax.Precision.HIGHEST)
    heads_out = (near_out + far_out).astype(jnp.bfloat16).reshape(span, width)
    return lax.psum_scatter(
        jnp.dot(heads_out, w_out, preferred_element_type=jnp.float32).astype(jnp.bfloat16),
        "head",
        scatter_dimension=0,
        tiled=True,
    )


def solution(mesh):
    in_specs = (
        P(("ctx", "head"), None),
        P("ctx", "head"),
        P("ctx", "head"),
        P("ctx", "head"),
        P("head", None),
        P("head", "ctx"),
        P("head", None),
        P("ctx", None),
    )
    out_specs = P(("ctx", "head"), None)
    return jax.shard_map(
        on_device, mesh=mesh, in_specs=in_specs, out_specs=out_specs, check_vma=False
    )
```

profile of v0, /device:TPU:0, one launch (start us, length us, event | category | flops | bytes accessed | tf_op | source)
XLA Modules:
  0.0 354.7 jit_solution(5729758578422168812)
XLA Ops:
  6.5 0.7 all-gather.5.cloned.1.call-update
  7.3 0.7 all-gather.9.cloned.1.call-update
  8.1 0.7 all-gather.11.cloned.1.call-update
  8.8 0.5 all-gather.7.cloned.1.call-update
  9.4 0.7 reshape.199
  10.1 1.2 reduce-window.6
  11.3 0.1 slice.12
  11.3 0.1 copy.19
  11.5 0.1 copy.20
  11.6 0.1 add_bitcast_fusion
  11.7 0.1 slice.13
  11.7 0.1 copy.39
  11.8 3.1 collective-permute-start.1
  14.9 0.7 convert_element_type.227
  15.6 0.1 fusion.73
  15.7 0.9 convolution_bitcast_fusion.2
  16.6 0.1 copy.21
  16.7 0.1 copy.24
  16.9 0.1 copy.27
  17.0 0.9 fusion.33
  17.9 0.1 broadcast_in_dim.27
  18.0 0.2 copy.40
  18.2 0.3 mul.82
  18.5 0.8 mul.83
  19.4 20.3 %all-gather.5.cloned.1.call-done = bf16[256,4096]{1,0:T(8,128)(2,1)} async-done(((bf16[32,4096]{1,0:T(8,128)(2,1)}), bf16[256,4096]{1,0:T(8,128)(2,1)}) %all-gather.5.cloned.1.call-update) | async-done | bytes 2097168 | tf_op jit(solution)/shard_map/all_gather | solution.py:37
  39.8 82.3 %all-gather.9.cloned.1.call-done = bf16[4096,512]{1,0:T(8,128)(2,1)} async-done(((bf16[1024,512]{1,0:T(8,128)(2,1)}), bf16[4096,512]{1,0:T(8,128)(2,1)}) %all-gather.9.cloned.1.call-update) | async-done | bytes 4194320 | tf_op jit(solution)/shard_map/all_gather | solution.py:33
  122.1 4.1 %fusion.7 = f32[256,512]{1,0:T(8,128)S(1)} fusion(bf16[256,4096]{1,0:T(8,128)(2,1)} %all-gather.5.cloned.1.call-done, bf16[4096,512]{1,0:T(8,128)(2,1)} %all-gather.9.cloned.1.call-done), kind=kOutput, calls=%fused_computation.13 | convolution fusion | flops 1074003968 | bytes 6815744 | tf_op jit(solution)/shard_map/dot_general | solution.py:39
  126.2 0.2 reshape.203
  126.3 76.6 %all-gather.11.cloned.1.call-done = bf16[4096,512]{1,0:T(8,128)(2,1)} async-done(((bf16[1024,512]{1,0:T(8,128)(2,1)}), bf16[4096,512]{1,0:T(8,128)(2,1)}) %all-gather.11.cloned.1.call-update) | async-done | bytes 4194320 | tf_op jit(solution)/shard_map/all_gather | solution.py:34
  202.9 4.1 %fusion.6 = f32[256,512]{1,0:T(8,128)S(1)} fusion(bf16[256,4096]{1,0:T(8,128)(2,1)} %all-gather.5.cloned.1.call-done, bf16[4096,512]{1,0:T(8,128)(2,1)} %all-gather.11.cloned.1.call-done), kind=kOutput, calls=%fused_computation.11 | convolution fusion | flops 1074003968 | bytes 6815744 | tf_op jit(solution)/shard_map/dot_general | solution.py:39
  207.0 0.2 reshape.204
  207.2 0.3 multiply_reduce_fusion
  207.5 0.3 multiply_reduce_fusion.1
  207.9 0.7 multiply_convert_fusion
  208.6 75.0 %all-gather.7.cloned.1.call-done = bf16[4096,512]{1,0:T(8,128)(2,1)} async-done(((bf16[1024,512]{1,0:T(8,128)(2,1)}), bf16[4096,512]{1,0:T(8,128)(2,1)}) %all-gather.7.cloned.1.call-update) | async-done | bytes 4194320 | tf_op jit(solution)/shard_map/all_gather | solution.py:35
  283.6 4.1 %fusion.8 = bf16[32,4,8,128]{3,2,1,0:T(8,128)(2,1)S(1)} fusion(bf16[256,4096]{1,0:T(8,128)(2,1)} %all-gather.5.cloned.1.call-done, bf16[4096,512]{1,0:T(8,128)(2,1)} %all-gather.7.cloned.1.call-done), kind=kOutput, calls=%fused_computation.15 | convolution fusion | flops 1073872896 | bytes 6553600 | tf_op jit(solution)/shard_map/dot_general | solution.py:39
  287.7 0.3 fusion.87
  288.0 0.1 collective-permute-start
  288.1 5.0 %collective-permute-done = bf16[4,128,128]{2,1,0:T(8,128)(2,1)S(1)} collective-permute-done((bf16[4,128,128]{2,1,0:T(8,128)(2,1)S(1)}, bf16[4,128,128]{2,1,0:T(8,128)(2,1)S(1)}, u32[]{:S(2)}, u32[]{:S(2)}) %collective-permute-start) | collective-permute-done | bytes 131104 | tf_op jit(solution)/shard_map/ppermute | solution.py:13
  293.1 0.1 fusion.19
  293.2 0.9 collective-permute-start.2
  294.2 0.7 multiply_bitcast_fusion
  294.9 6.4 %collective-permute-done.2 = bf16[4,128,128]{2,1,0:T(8,128)(2,1)S(1)} collective-permute-done((bf16[4,128,128]{2,1,0:T(8,128)(2,1)S(1)}, bf16[4,128,128]{2,1,0:T(8,128)(2,1)S(1)}, u32[]{:S(2)}, u32[]{:S(2)}) %collective-permute-start.2) | collective-permute-done | bytes 131104 | tf_op jit(solution)/shard_map/ppermute | solution.py:13
  301.2 0.1 select_bitcast_fusion
  301.3 1.1 fusion.3
  302.4 0.6 fusion.5
  303.0 4.8 %convolution_convert_fusion = bf16[256,4096]{1,0:T(8,128)(2,1)} fusion(bf16[256,512]{0,1:T(8,128)(2,1)S(1)} %bitcast.57, bf16[512,4096]{1,0:T(8,128)(2,1)} %param.12), kind=kOutput, calls=%fused_computation | convolution fusion | flops 1074790400 | bytes 6553600 | tf_op jit(solution)/shard_map/dot_general | solution.py:107
  307.9 40.3 %reduce-scatter.2.cloned.1.call-done = bf16[32,4096]{1,0:T(8,128)(2,1)} async-done(((bf16[256,4096]{1,0:T(8,128)(2,1)}), bf16[32,4096]{1,0:T(8,128)(2,1)}) %reduce-scatter.2.cloned.1.call-update) | async-done | bytes 262160 | tf_op jit(solution)/shard_map/reduce_scatter | solution.py:106
  (17 shorter events, 0.4 us)
Async XLA Ops:
  6.5 33.2 %all-gather.5.cloned.1.call-start = ((), (), s32[]{:S(2)}) async-start(), calls=%async_computation.1 | async-start | bytes 2359296 | tf_op jit(solution)/shard_map/all_gather | solution.py:37
  7.3 114.8 %all-gather.9.cloned.1.call-start = ((), (), s32[]{:S(2)}) async-start(), calls=%async_computation.3 | async-start | bytes 5242880 | tf_op jit(solution)/shard_map/all_gather | solution.py:33
  8.0 194.9 %all-gather.11.cloned.1.call-start = ((), (), s32[]{:S(2)}) async-start(), calls=%async_computation.4 | async-start | bytes 5242880 | tf_op jit(solution)/shard_map/all_gather | solution.py:34
  8.7 274.9 %all-gather.7.cloned.1.call-start = ((), (), s32[]{:S(2)}) async-start(), calls=%async_computation.2 | async-start | bytes 5242880 | tf_op jit(solution)/shard_map/all_gather | solution.py:35
  9.3 338.8 %reduce-scatter.2.cloned.1.call-start = ((), (), s32[]{:S(2)}) async-start(), calls=%async_computation.5 | async-start | bytes 2359296 | tf_op jit(solution)/shard_map/reduce_scatter | solution.py:106
  11.8 7.6 %collective-permute-start.1 = (bf16[4]{0:T(256)(128)(2,1)S(1)}, bf16[4]{0:T(256)(128)(2,1)S(1)}, u32[]{:S(2)}, u32[]{:S(2)}) collective-permute-start(bf16[4]{0:T(256)(128)(2,1)S(1)} %bitcast_convert_fusion), channel_id=1, source_target_pairs={{0,8},{8,0},{16,24},{24,16},{1,9},{9,1},{17,25},{25,17},{2,10},{10... | collective-permute-start | bytes 32 | tf_op jit(solution)/shard_map/ppermute | solution.py:13
  288.0 5.2 %collective-permute-start = (bf16[4,128,128]{2,1,0:T(8,128)(2,1)S(1)}, bf16[4,128,128]{2,1,0:T(8,128)(2,1)S(1)}, u32[]{:S(2)}, u32[]{:S(2)}) collective-permute-start(bf16[4,128,128]{2,1,0:T(8,128)(2,1)S(1)} %get-tuple-element.17), channel_id=1, source_target_pairs={{0,8},{8,0},{16,24},{24,16},{1,9},{9,1},{17,25},{25,17},{2,10},{10... | collective-permute-start | bytes 393224 | tf_op jit(solution)/shard_map/ppermute | solution.py:13
  293.2 8.0 %collective-permute-start.2 = (bf16[4,128,128]{2,1,0:T(8,128)(2,1)S(1)}, bf16[4,128,128]{2,1,0:T(8,128)(2,1)S(1)}, u32[]{:S(2)}, u32[]{:S(2)}) collective-permute-start(bf16[4,128,128]{2,1,0:T(8,128)(2,1)S(1)} %get-tuple-element.10), channel_id=1, source_target_pairs={{0,16},{8,24},{16,0},{24,8},{1,17},{9,25},{17,1},{25,9},{2,18},{10... | collective-permute-start | bytes 393224 | tf_op jit(solution)/shard_map/ppermute | solution.py:13
Sparse Core Ops, SparseCore 0:
  9.2 30.4 all-gather.4
  41.3 80.7 all-gather.8
  123.7 79.2 all-gather.10
  204.3 79.2 all-gather.6
  308.0 40.1 reduce-scatter.1
where the time goes:
time: 355 us
  waiting for transfers between devices  308 us (87%)
  matrix products  20.7 us (6%)
  between operations  13.3 us (4%)
  other arithmetic  4.58 us (1%)
  starting transfers between devices  4.23 us (1%)
    all_gather x1, waiting for transfers between devices, on_device(): lax.all_gather(w_query, 'ctx', axis=0, tiled=True)  82.3 us
    all_gather x1, waiting for transfers between devices, on_device(): lax.all_gather(w_key, 'ctx', axis=0, tiled=True)  76.6 us
    all_gather x1, waiting for transfers between devices, on_device(): lax.all_gather(w_value, 'ctx', axis=0, tiled=True)  75 us
    reduce_scatter x1, waiting for transfers between devices, on_device(): lax.psum_scatter(jnp.dot(heads_out, w_out, preferred_element_type=jnp.flo...  40.3 us
    all_gather x1, waiting for transfers between devices, on_device(): piece = lax.all_gather(layer_input, 'head', axis=0, tiled=True)  20.3 us
    dot_general x3, matrix products, on_device(): jnp.dot(piece, weight, preferred_element_type=jnp.float32)  12.2 us
    ppermute x3, waiting for transfers between devices, swapped(): return lax.ppermute(value, axis, pairs)  11.4 us
  transfers between devices with their start and end apart: 8, of which 7 were waited for; matrix products, arithmetic and copies ran while one was open for 5% of the time, Pallas kernels for 0%

commit v1 on v0

--- a/solution.py
+++ b/solution.py
@@ -5,6 +5,14 @@
 
 HEAD_DIM = 128
 BLOCK = 128
+
+
+def sections_proceed(inputs, axis_k):
+    inputs = jnp.moveaxis(inputs, 0, axis_k)
+    placed = inputs.shape
+    return inputs.reshape(
+        *placed[:axis_k], placed[axis_k] * placed[axis_k + 1], *placed[axis_k + 2 :]
+    )
 
 
 def swapped(value, axis, stride):
@@ -29,8 +37,19 @@
 
 
 def on_device(layer_input, w_query, w_key, w_value, w_out, log_decay, level_gain, level_mask):
+
+    def list_yards(local_block, peer_axis, on_dim):
+        slots = lax.axis_size(peer_axis)
+        history = [(to_i, (to_i + 1) % slots) for to_i in range(slots)]
+        series = [local_block]
+        while len(series) < slots:
+            series.append(lax.ppermute(series[-1], axis_name=peer_axis, perm=history))
+        b_now = lax.axis_index(peer_axis)
+        series = jnp.stack(series, 0)[(b_now - jnp.arange(slots)) % slots]
+        return sections_proceed(series, on_dim)
+
     full_query, full_key, full_value = (
-        lax.all_gather(w_query, "ctx", axis=0, tiled=True),
+        list_yards(w_query, "ctx", 0),
         lax.all_gather(w_key, "ctx", axis=0, tiled=True),
         lax.all_gather(w_value, "ctx", axis=0, tiled=True),
     )

time: 355 us -> 306 us (0.86)
  waiting for transfers between devices: 308 us -> 248 us
  starting transfers between devices: 4.23 us -> 10.9 us
  local copies, waits for them, and re-layouts: 3.36 us -> 8.11 us
    ppermute x0 -> x3, waiting for transfers between devices: none -> 103 us  [list_yards(): series.append(lax.ppermute(series[-1], axis_name=peer_axis, perm=history))]
    all_gather x1 -> x0, waiting for transfers between devices: 82.3 us -> none  [on_device(): lax.all_gather(w_query, 'ctx', axis=0, tiled=True)]
    all_gather x1, waiting for transfers between devices: 76.6 us -> 16.4 us  [on_device(): lax.all_gather(w_key, 'ctx', axis=0, tiled=True)]
    all_gather x1, waiting for transfers between devices: 20.3 us -> 0.01 us  [on_device(): piece = lax.all_gather(layer_input, 'head', axis=0, tiled=True)]
    ppermute x0 -> x3, starting transfers between devices: none -> 8.49 us  [list_yards(): series.append(lax.ppermute(series[-1], axis_name=peer_axis, perm=history))]
    gather x0 -> x1, local copies, waits for them, and re-layouts: none -> 4.93 us  [list_yards(): series = jnp.stack(series, 0)[(b_now - jnp.arange(slots)) % slots]]
    another operation x2 -> x3, other arithmetic: 1.24 us -> 4.87 us  [the longest x1 3.62 us: list_yards(): series = jnp.stack(series, 0)[(b_now - jnp.arange(slots)) % slots]]
  transfers between devices with their start and end apart: 8 -> 10, of which waited for: 7 -> 8; matrix products, arithmetic and copies ran while one was open for 5% -> 7% of each run, Pallas kernels for 0% -> 0%
where the time goes in v1:
time: 306 us
  waiting for transfers between devices  248 us (81%)
  matrix products  18.2 us (6%)
  between operations  13.3 us (4%)
  starting transfers between devices  10.9 us (4%)
  local copies, waits for them, and re-layouts  8.11 us (3%)
  other arithmetic  7.15 us (2%)
    ppermute x3, waiting for transfers between devices, list_yards(): series.append(lax.ppermute(series[-1], axis_name=peer_axis, perm=history))  103 us
    all_gather x1, waiting for transfers between devices, on_device(): lax.all_gather(w_value, 'ctx', axis=0, tiled=True)  75.1 us
    reduce_scatter x1, waiting for transfers between devices, on_device(): lax.psum_scatter(jnp.dot(heads_out, w_out, preferred_element_type=jnp.flo...  40.3 us
    all_gather x1, waiting for transfers between devices, on_device(): lax.all_gather(w_key, 'ctx', axis=0, tiled=True)  16.4 us
    ppermute x3, waiting for transfers between devices, swapped(): return lax.ppermute(value, axis, pairs)  10.7 us
    dot_general x3, matrix products, on_device(): jnp.dot(piece, weight, preferred_element_type=jnp.float32)  9.6 us
    ppermute x3, starting transfers between devices, list_yards(): series.append(lax.ppermute(series[-1], axis_name=peer_axis, perm=history))  8.49 us
  transfers between devices with their start and end apart: 10, of which 8 were waited for; matrix products, arithmetic and copies ran while one was open for 7% of the time, Pallas kernels for 0%

profile of v1, /device:TPU:0, one launch (start us, length us, event | category | flops | bytes accessed | tf_op | source)
XLA Modules:
  0.0 305.5 jit_solution(434607616284865945)
XLA Ops:
  6.5 0.7 all-gather.4.cloned.1.call-update
  7.3 0.7 all-gather.8.cloned.1.call-update
  8.1 0.7 all-gather.6.cloned.1.call-update
  8.8 3.1 %collective-permute-start = (bf16[1024,512]{1,0:T(8,128)(2,1)}, bf16[1024,512]{1,0:T(8,128)(2,1)S(1)}, u32[]{:S(2)}, u32[]{:S(2)}) collective-permute-start(bf16[1024,512]{1,0:T(8,128)(2,1)} %param.9), channel_id=1, source_target_pairs={{0,8},{8,16},{16,24},{24,0},{1,9},{9,17},{17,25},{25,1},{2,10},{10... | collective-permute-start | bytes 3145736 | tf_op jit(solution)/shard_map/ppermute | solution.py:46
  11.9 25.4 %collective-permute-done = bf16[1024,512]{1,0:T(8,128)(2,1)S(1)} collective-permute-done((bf16[1024,512]{1,0:T(8,128)(2,1)}, bf16[1024,512]{1,0:T(8,128)(2,1)S(1)}, u32[]{:S(2)}, u32[]{:S(2)}) %collective-permute-start) | collective-permute-done | bytes 1048608 | tf_op jit(solution)/shard_map/ppermute | solution.py:46
  37.3 0.7 reshape.252
  38.0 1.2 reduce-window.6
  39.2 0.1 slice.14
  39.3 0.1 copy.31
  39.4 0.1 copy.32
  39.5 0.1 add_bitcast_fusion
  39.6 0.1 slice.15
  39.7 0.1 copy.54
  39.8 1.3 collective-permute-start.4
  41.1 0.7 convert_element_type.232
  41.8 0.1 fusion.74
  41.8 32.6 %collective-permute-done.1 = bf16[1024,512]{1,0:T(8,128)(2,1)} collective-permute-done((bf16[1024,512]{1,0:T(8,128)(2,1)S(1)}, bf16[1024,512]{1,0:T(8,128)(2,1)}, u32[]{:S(2)}, u32[]{:S(2)}) %collective-permute-start.1) | collective-permute-done | bytes 1048608 | tf_op jit(solution)/shard_map/ppermute | solution.py:46
  74.5 5.4 %collective-permute-start.2 = (bf16[1024,512]{1,0:T(8,128)(2,1)}, bf16[1024,512]{1,0:T(8,128)(2,1)}, u32[]{:S(2)}, u32[]{:S(2)}) collective-permute-start(bf16[1024,512]{1,0:T(8,128)(2,1)} %collective-permute-done.1), channel_id=1, source_target_pairs={{0,8},{8,16},{16,24},{24,0},{1,9},{9,17},{17,25},{25,1},{2,10},{10... | collective-permute-start | bytes 3145736 | tf_op jit(solution)/shard_map/ppermute | solution.py:46
  79.9 0.9 fusion.34
  80.7 0.1 broadcast_in_dim.27
  80.8 0.2 copy.55
  81.1 0.2 copy.36
  81.3 0.9 convolution_bitcast_fusion.2
  82.1 0.1 copy.33
  82.2 0.3 mul.82
  82.6 0.8 mul.83
  83.5 45.3 %collective-permute-done.2 = bf16[1024,512]{1,0:T(8,128)(2,1)} collective-permute-done((bf16[1024,512]{1,0:T(8,128)(2,1)}, bf16[1024,512]{1,0:T(8,128)(2,1)}, u32[]{:S(2)}, u32[]{:S(2)}) %collective-permute-start.2) | collective-permute-done | bytes 1048608 | tf_op jit(solution)/shard_map/ppermute | solution.py:46
  128.9 3.6 %pad_maximum_fusion = bf16[4,1024,512]{2,1,0:T(8,128)(2,1)} fusion(bf16[1,1024,512]{2,1,0:T(8,128)(2,1)} %bitcast.3, bf16[1,1024,512]{2,1,0:T(8,128)(2,1)} %bitcast.2, bf16[1,1024,512]{2,1,0:T(8,128)(2,1)} %bitcast.79, bf16[1,1024,512]{2,1,0:T(8,128)(2,1)S(1)} %bitcast.78), kind=kLoop, calls=%fused_computation.2 | loop fusion | flops 6291456 | bytes 8388608 | tf_op jit(solution)/shard_map/stack | solution.py:48
  132.5 4.9 %gather_fusion = bf16[4,1024,512]{2,1,0:T(8,128)(2,1)} fusion(bf16[4,1024,512]{2,1,0:T(8,128)(2,1)} %pad_maximum_fusion, s32[1024]{0:T(1024)S(1)} %pad_clamp_fusion), kind=kCustom, calls=%fused_computation | custom fusion | bytes 8388624 | tf_op jit(solution)/shard_map/gather | solution.py:48
  137.4 16.4 %all-gather.8.cloned.1.call-done = bf16[4096,512]{1,0:T(8,128)(2,1)} async-done(((bf16[1024,512]{1,0:T(8,128)(2,1)}), bf16[4096,512]{1,0:T(8,128)(2,1)}) %all-gather.8.cloned.1.call-update) | async-done | bytes 4194320 | tf_op jit(solution)/shard_map/all_gather | solution.py:53
  153.8 4.1 %fusion.6 = f32[256,512]{1,0:T(8,128)S(1)} fusion(bf16[256,4096]{1,0:T(8,128)(2,1)} %all-gather.4.cloned.1.call-done, bf16[4096,512]{1,0:T(8,128)(2,1)} %all-gather.8.cloned.1.call-done), kind=kOutput, calls=%fused_computation.13 | convolution fusion | flops 1074003968 | bytes 6815744 | tf_op jit(solution)/shard_map/dot_general | solution.py:58
  157.9 0.2 reshape.257
  158.1 0.3 multiply_reduce_fusion
  158.5 0.7 multiply_convert_fusion
  159.2 75.1 %all-gather.6.cloned.1.call-done = bf16[4096,512]{1,0:T(8,128)(2,1)} async-done(((bf16[1024,512]{1,0:T(8,128)(2,1)}), bf16[4096,512]{1,0:T(8,128)(2,1)}) %all-gather.6.cloned.1.call-update) | async-done | bytes 4194320 | tf_op jit(solution)/shard_map/all_gather | solution.py:54
  234.3 4.2 %fusion.8 = bf16[32,4,8,128]{3,2,1,0:T(8,128)(2,1)S(1)} fusion(bf16[256,4096]{1,0:T(8,128)(2,1)} %all-gather.4.cloned.1.call-done, bf16[4096,512]{1,0:T(8,128)(2,1)} %all-gather.6.cloned.1.call-done), kind=kOutput, calls=%fused_computation.17 | convolution fusion | flops 1073872896 | bytes 6553600 | tf_op jit(solution)/shard_map/dot_general | solution.py:58
  238.5 0.3 fusion.90
  238.8 0.1 copy-done.3
  239.0 1.3 multiply_reduce_fusion.1
  240.3 3.6 %collective-permute-done.3 = bf16[4,128,128]{2,1,0:T(8,128)(2,1)S(1)} collective-permute-done((bf16[4,128,128]{2,1,0:T(8,128)(2,1)S(1)}, bf16[4,128,128]{2,1,0:T(8,128)(2,1)S(1)}, u32[]{:S(2)}, u32[]{:S(2)}) %collective-permute-start.3) | collective-permute-done | bytes 131104 | tf_op jit(solution)/shard_map/ppermute | solution.py:21
  243.9 0.1 fusion.21
  244.0 0.9 collective-permute-start.5
  245.0 7.1 %collective-permute-done.5 = bf16[4,128,128]{2,1,0:T(8,128)(2,1)S(1)} collective-permute-done((bf16[4,128,128]{2,1,0:T(8,128)(2,1)S(1)}, bf16[4,128,128]{2,1,0:T(8,128)(2,1)S(1)}, u32[]{:S(2)}, u32[]{:S(2)}) %collective-permute-start.5) | collective-permute-done | bytes 131104 | tf_op jit(solution)/shard_map/ppermute | solution.py:21
  252.0 0.1 select_bitcast_fusion
  252.1 1.1 fusion.3
  253.2 0.7 fusion.5
  253.9 4.8 %convolution_convert_fusion = bf16[256,4096]{1,0:T(8,128)(2,1)} fusion(bf16[256,512]{0,1:T(8,128)(2,1)S(1)} %bitcast.80, bf16[512,4096]{1,0:T(8,128)(2,1)} %param.12), kind=kOutput, calls=%fused_computation.1 | convolution fusion | flops 1074790400 | bytes 6553600 | tf_op jit(solution)/shard_map/dot_general | solution.py:126
  258.7 40.3 %reduce-scatter.2.cloned.1.call-done = bf16[32,4096]{1,0:T(8,128)(2,1)} async-done(((bf16[256,4096]{1,0:T(8,128)(2,1)}), bf16[32,4096]{1,0:T(8,128)(2,1)}) %reduce-scatter.2.cloned.1.call-update) | async-done | bytes 262160 | tf_op jit(solution)/shard_map/reduce_scatter | solution.py:125
  (28 shorter events, 0.5 us)
Async XLA Ops:
  6.5 122.3 %copy-start.1 = (bf16[1024,512]{1,0:T(8,128)(2,1)S(1)}, bf16[1024,512]{1,0:T(8,128)(2,1)}, u32[]{:S(2)}) copy-start(bf16[1024,512]{1,0:T(8,128)(2,1)} %param.9) | copy-start | bytes 3145732
  6.5 130.9 %all-gather.4.cloned.1.call-start = ((), (), s32[]{:S(2)}) async-start(), calls=%async_computation.1 | async-start | bytes 2359296 | tf_op jit(solution)/shard_map/all_gather | solution.py:56
  7.3 146.6 %all-gather.8.cloned.1.call-start = ((), (), s32[]{:S(2)}) async-start(), calls=%async_computation.3 | async-start | bytes 5242880 | tf_op jit(solution)/shard_map/all_gather | solution.py:53
  8.0 226.2 %all-gather.6.cloned.1.call-start = ((), (), s32[]{:S(2)}) async-start(), calls=%async_computation.2 | async-start | bytes 5242880 | tf_op jit(solution)/shard_map/all_gather | solution.py:54
  8.7 290.2 %reduce-scatter.2.cloned.1.call-start = ((), (), s32[]{:S(2)}) async-start(), calls=%async_computation.4 | async-start | bytes 2359296 | tf_op jit(solution)/shard_map/reduce_scatter | solution.py:125
  8.8 28.5 %collective-permute-start = (bf16[1024,512]{1,0:T(8,128)(2,1)}, bf16[1024,512]{1,0:T(8,128)(2,1)S(1)}, u32[]{:S(2)}, u32[]{:S(2)}) collective-permute-start(bf16[1024,512]{1,0:T(8,128)(2,1)} %param.9), channel_id=1, source_target_pairs={{0,8},{8,16},{16,24},{24,0},{1,9},{9,17},{17,25},{25,1},{2,10},{10... | collective-permute-start | bytes 3145736 | tf_op jit(solution)/shard_map/ppermute | solution.py:46
  37.3 42.6 %copy-start.2 = (bf16[1024,512]{1,0:T(8,128)(2,1)}, bf16[1024,512]{1,0:T(8,128)(2,1)S(1)}, u32[]{:S(2)}) copy-start(bf16[1024,512]{1,0:T(8,128)(2,1)S(1)} %collective-permute-done) | copy-start | bytes 3145732
  37.3 37.2 %collective-permute-start.1 = (bf16[1024,512]{1,0:T(8,128)(2,1)S(1)}, bf16[1024,512]{1,0:T(8,128)(2,1)}, u32[]{:S(2)}, u32[]{:S(2)}) collective-permute-start(bf16[1024,512]{1,0:T(8,128)(2,1)S(1)} %collective-permute-done), channel_id=1, source_target_pairs={{0,8},{8,16},{16,24},{24,0},{1,9},{9,17},{17,25},{25,1},{2,10},{10... | collective-permute-start | bytes 3145736 | tf_op jit(solution)/shard_map/ppermute | solution.py:46
  39.8 43.7 %collective-permute-start.4 = (bf16[4]{0:T(256)(128)(2,1)S(1)}, bf16[4]{0:T(256)(128)(2,1)S(1)}, u32[]{:S(2)}, u32[]{:S(2)}) collective-permute-start(bf16[4]{0:T(256)(128)(2,1)S(1)} %bitcast_convert_fusion), channel_id=1, source_target_pairs={{0,8},{8,0},{16,24},{24,16},{1,9},{9,1},{17,25},{25,17},{2,10},{10... | collective-permute-start | bytes 32 | tf_op jit(solution)/shard_map/ppermute | solution.py:21
  74.5 54.4 %collective-permute-start.2 = (bf16[1024,512]{1,0:T(8,128)(2,1)}, bf16[1024,512]{1,0:T(8,128)(2,1)}, u32[]{:S(2)}, u32[]{:S(2)}) collective-permute-start(bf16[1024,512]{1,0:T(8,128)(2,1)} %collective-permute-done.1), channel_id=1, source_target_pairs={{0,8},{8,16},{16,24},{24,0},{1,9},{9,17},{17,25},{25,1},{2,10},{10... | collective-permute-start | bytes 3145736 | tf_op jit(solution)/shard_map/ppermute | solution.py:46
  234.2 4.6 %copy-start = (bf16[4,1024,512]{2,1,0:T(8,128)(2,1)S(1)}, bf16[4,1024,512]{2,1,0:T(8,128)(2,1)}, u32[]{:S(2)}) copy-start(bf16[4,1024,512]{2,1,0:T(8,128)(2,1)} %gather_fusion) | copy-start | bytes 12582916
  234.3 4.7 %copy-start.3 = (bf16[256,4096]{1,0:T(8,128)(2,1)S(1)}, bf16[256,4096]{1,0:T(8,128)(2,1)}, u32[]{:S(2)}) copy-start(bf16[256,4096]{1,0:T(8,128)(2,1)} %all-gather.4.cloned.1.call-done) | copy-start | bytes 6291460
  238.7 5.2 %collective-permute-start.3 = (bf16[4,128,128]{2,1,0:T(8,128)(2,1)S(1)}, bf16[4,128,128]{2,1,0:T(8,128)(2,1)S(1)}, u32[]{:S(2)}, u32[]{:S(2)}) collective-permute-start(bf16[4,128,128]{2,1,0:T(8,128)(2,1)S(1)} %get-tuple-element.15), channel_id=1, source_target_pairs={{0,8},{8,0},{16,24},{24,16},{1,9},{9,1},{17,25},{25,17},{2,10},{10... | collective-permute-start | bytes 393224 | tf_op jit(solution)/shard_map/ppermute | solution.py:21
  244.0 8.0 %collective-permute-start.5 = (bf16[4,128,128]{2,1,0:T(8,128)(2,1)S(1)}, bf16[4,128,128]{2,1,0:T(8,128)(2,1)S(1)}, u32[]{:S(2)}, u32[]{:S(2)}) collective-permute-start(bf16[4,128,128]{2,1,0:T(8,128)(2,1)S(1)} %get-tuple-element.8), channel_id=1, source_target_pairs={{0,16},{8,24},{16,0},{24,8},{1,17},{9,25},{17,1},{25,9},{2,18},{10... | collective-permute-start | bytes 393224 | tf_op jit(solution)/shard_map/ppermute | solution.py:21
Sparse Core Ops, SparseCore 0:
  9.2 30.5 all-gather.3
  41.4 112.3 all-gather.7
  155.4 78.8 all-gather.5
  258.8 40.1 reduce-scatter.1
